TPU v7x, 256 devices: a whole 4x4x8 slice. The times are simulated.
256 devices in a mesh: section: 8 (over z), expert: 8 (over y_hi, x), dp: 4 (over y_lo, core).
Axes of the slice: x: 4, y: 4 (y_hi: 2, y_lo: 2; y = y_hi * 2 + y_lo), z: 8, core: 2. Of those that a mesh axis runs over, the one named last changes fastest.
Arguments:
- tokens: bfloat16 [8, 256, 4096], P('section', None, ('expert', 'dp'))
- targets: bfloat16 [8, 256, 4096], P('section', None, ('expert', 'dp')), may hold values from -6 to 6
- group_ids: int32 [8, 256], P('section'), may hold values from 0 to 7, as said below
- expert_ids: int32 [1, 8, 8, 256, 2], P(None, 'section'), may hold values from 0 to 7, all different within a row; in each aligned block of 256 rows (0 to 255, 256 to 511, ..., all dimensions but the last counted through in order) at most 72 rows name the same one
- norm_gain: float32 [8, 4096], P('section', ('expert', 'dp')), may hold values from 0.5 to 1.5
- router: bfloat16 [8, 4096, 8], P('section', ('expert', 'dp')), may hold values from -0.09375 to 0.09375
- w_gate: bfloat16 [8, 8, 4096, 1536], P('section', 'expert', None, 'dp'), may hold values from -0.09375 to 0.09375
- w_up: bfloat16 [8, 8, 4096, 1536], P('section', 'expert', None, 'dp'), may hold values from -0.09375 to 0.09375
- w_down: bfloat16 [8, 8, 1536, 4096], P('section', 'expert', 'dp'), may hold values from -0.15625 to 0.15625
Outputs:
- grad_out: bfloat16 [8, 256, 4096], P('section', None, ('expert', 'dp'))
- group_loss: float32 [8], replicated
Inputs may be any that keep to these rules, and one draw needn't show every extreme that they name: `expert_ids`: in each aligned block of 256 rows (one micro-batch at one layer pass) no expert is named by more than 72 rows; a row names 2 different experts. `group_ids`: exactly one group has no rows; which one varies.
All inputs are finite; a program needn't handle non-finite values.
Results may differ from a plain program's by a relative error of at most 0.019.
Values may be sent and summed in bfloat16 or wider, within the bound.
A program may use at most 64 MiB of HBM per device.

v0:
```python
import jax
import jax.numpy as jnp
from jax import lax
from jax.sharding import PartitionSpec as P

GROUPS = 8
dro_rate = 0.3


def from_behind(value, axis, steps):
    count = lax.axis_size(axis)
    pairs = [(source, (source + steps) % count) for source in range(count)]
    return lax.ppermute(value, axis, pairs)


def per_device(tokens, targets, group_ids, expert_ids, norm_gain, router, w_gate, w_up, w_down):
    sections = lax.axis_size("section")
    lane_count = lax.axis_size("dp")
    experts = lax.axis_size("expert")
    circuits = expert_ids.shape[0]
    top_count = expert_ids.shape[-1]
    row_count = tokens.shape[1]
    piece_width = tokens.shape[2]
    full_width = piece_width * experts * lane_count
    capacity = min(row_count, row_count * top_count // experts * 9 // 8)
    section_place = lax.axis_index("section")
    gain_row = norm_gain[0]
    router_block = router[0]
    gate_matrix = w_gate[0, 0]
    up_matrix = w_up[0, 0]
    down_matrix = w_down[0, 0]
    expert_range = jnp.arange(experts, dtype=jnp.int32)
    slot_range = jnp.arange(capacity, dtype=jnp.int32)
    zero_index = jnp.zeros((), jnp.int32)

    def expert_rows(flat_rows):
        gate_part = jnp.dot(flat_rows, gate_matrix, preferred_element_type=jnp.float32)
        up_part = jnp.dot(flat_rows, up_matrix, preferred_element_type=jnp.float32)
        activated = (jax.nn.silu(gate_part) * up_part).astype(jnp.bfloat16)
        return jnp.dot(activated, down_matrix, preferred_element_type=jnp.float32).astype(
            jnp.bfloat16
        )

    def joined_work(received):
        item_count = received.shape[1]
        expert_part = expert_rows(received.reshape(item_count, full_width))
        return lax.all_to_all(
            expert_part.reshape(item_count, experts * lane_count, piece_width),
            ("expert", "dp"),
            split_axis=1,
            concat_axis=1,
            tiled=True,
        )

    def one_tick(moment, current):
        micro_index = (section_place - moment) % sections
        circuit = (moment // sections).astype(jnp.int32)
        choices = lax.dynamic_slice(
            expert_ids,
            (circuit, zero_index, micro_index, zero_index, zero_index),
            (1, 1, 1, row_count, top_count),
        ).reshape(row_count, top_count)
        wide_state = current.astype(jnp.float32)
        local_squares = jnp.sum(wide_state * wide_state, axis=1)
        total_squares = lax.psum(local_squares, ("expert", "dp"))
        row_scale = lax.rsqrt(total_squares / full_width + 1e-06)[:, None]
        normed = (wide_state * row_scale * gain_row[None, :]).astype(jnp.bfloat16)
        partial_logits = jnp.dot(normed, router_block, preferred_element_type=jnp.float32)
        logits = lax.psum(partial_logits, ("expert", "dp"))
        member = (choices[:, :, None] == expert_range[None, None, :]).astype(jnp.int32)
        flat_member = member.reshape(-1, experts)
        rank_before = jnp.cumsum(flat_member, axis=0) - flat_member
        position = jnp.sum(rank_before * flat_member, axis=1).reshape(row_count, top_count)
        chosen = jnp.sum(logits[:, None, :] * member.astype(jnp.float32), axis=2)
        weights = jnp.exp(chosen)
        gate_weights = weights / jnp.sum(weights, axis=1, keepdims=True)
        placement = member.astype(jnp.float32)[:, :, :, None] * (
            position[:, :, None, None] == slot_range[None, None, None, :]
        ).astype(jnp.float32)
        picker = (
            jnp.sum(placement, axis=1).reshape(row_count, experts * capacity).astype(jnp.bfloat16)
        )
        combiner = jnp.sum(placement * gate_weights[:, :, None, None], axis=1)
        outgoing = jnp.einsum(
            "us,ud->sd", picker, normed, preferred_element_type=jnp.float32
        ).astype(jnp.bfloat16)
        spread = jnp.broadcast_to(
            outgoing.reshape(experts, 1, capacity, piece_width),
            (experts, lane_count, capacity, piece_width),
        )
        returned = joined_work(
            lax.all_to_all(
                spread.reshape(experts * lane_count, capacity, piece_width),
                ("expert", "dp"),
                split_axis=0,
                concat_axis=2,
                tiled=True,
            )
        )
        lane_total = jnp.sum(
            returned.reshape(capacity, experts, lane_count, piece_width).astype(jnp.float32), axis=2
        )
        mixture = jnp.einsum("uec,ced->ud", combiner, lane_total, precision=lax.Precision.HIGHEST)
        updated = (wide_state + mixture).astype(jnp.bfloat16)
        return from_behind(updated, "section", 1)

    final_state = lax.fori_loop(0, circuits * sections, one_tick, tokens[0])
    difference = final_state.astype(jnp.float32) - targets[0].astype(jnp.float32)
    partial_squares = jnp.sum(difference * difference, axis=1) / full_width
    group_member = (group_ids[0][:, None] == jnp.arange(GROUPS, dtype=jnp.int32)[None, :]).astype(
        jnp.float32
    )
    local_totals = jnp.dot(partial_squares, group_member, precision=lax.Precision.HIGHEST)
    first_lane = ((lax.axis_index("expert") == 0) & (lax.axis_index("dp") == 0)).astype(jnp.float32)
    local_counts = jnp.sum(group_member, axis=0) * first_lane
    totals, counts = lax.psum((local_totals, local_counts), ("section", "expert", "dp"))
    group_loss = totals / jnp.maximum(counts, 1.0)
    raised = jnp.exp(dro_rate * group_loss)
    group_weight = raised / jnp.sum(raised)
    token_count = sections * row_count
    row_weight_table = group_weight * token_count / jnp.maximum(counts, 1.0)
    row_weight = jnp.dot(group_member, row_weight_table, precision=lax.Precision.HIGHEST)
    grad_out = (row_weight[:, None] * difference).astype(jnp.bfloat16)[None]
    return (grad_out, group_loss)


def solution(mesh):
    placed = (
        P("section", None, ("expert", "dp")),
        P("section", None, ("expert", "dp")),
        P("section", None),
        P(None, "section", None, None, None),
        P("section", ("expert", "dp")),
        P("section", ("expert", "dp"), None),
        P("section", "expert", None, "dp"),
        P("section", "expert", None, "dp"),
        P("section", "expert", "dp", None),
    )
    return jax.shard_map(
        per_device,
        mesh=mesh,
        in_specs=placed,
        out_specs=(P("section", None, ("expert", "dp")), P()),
        check_vma=False,
    )
```

profile of v0, /device:TPU:1, one launch (start us, length us, event | category | flops | bytes accessed | tf_op | source)
XLA Modules:
  0.0 1500.4 jit_solution(1334823001441641367)
XLA Ops:
  2.3 1422.9 %while.17 = (s32[]{:T(128)}, bf16[256,128]{1,0:T(8,128)(2,1)S(1)}, s32[]{:T(128)}, s32[1,1,8,256,2]{3,4,2,1,0:T(2,128)}, f32[1,128]{1,0:T(1,128)}, /*index=5*/bf...) while((s32[]{:T(128)}, bf16[256,128]{1,0:T(8,128)(2,1)S(1)}, ...), condition=%wide.region_12.13_spmd.clone.clone, body=%wide.region_0.12_spmd.clone.clone.sunk | while | flops 947298688 | bytes 33643788 | solution.py:107
  4.3 65.3 %psum.50 = f32[256]{0:T(256)S(1)} all-reduce(f32[256]{0:T(256)S(1)} %fusion.92), channel_id=1, replica_groups=mesh['section'=8,'expert'=8,'dp'=4] {'expert','dp'}, use_global_device_ids=true, to_apply=%region_5.5 | all-reduce | flops 256 | bytes 2048 | tf_op jit(solution)/shard_map/while/body/eval_jaxpr/psum | solution.py:65
  70.4 66.5 %psum.51 = f32[256,8]{0,1:T(8,128)S(1)} all-reduce(f32[256,8]{0,1:T(8,128)S(1)} %fusion.93), channel_id=1, replica_groups=mesh['section'=8,'expert'=8,'dp'=4] {'expert','dp'}, use_global_device_ids=true, to_apply=%region_6.6 | all-reduce | flops 2048 | bytes 16384 | tf_op jit(solution)/shard_map/while/body/eval_jaxpr/psum | solution.py:69
  137.1 1.1 reduce-window.26
  140.3 15.9 %all_to_all.58 = bf16[32,72,128]{2,1,0:T(8,128)(2,1)S(1)} all-to-all(bf16[32,72,128]{2,1,0:T(8,128)(2,1)S(1)} %bitcast.117), channel_id=1, replica_groups=mesh['section'=8,'expert'=8,'dp'=4] {'expert','dp'}, dimensions={0} | all-to-all | bytes 1179648 | tf_op jit(solution)/shard_map/while/body/eval_jaxpr/all_to_all | solution.py:92
  157.0 4.4 fusion.95
  161.6 16.2 %all_to_all.59 = bf16[72,32,128]{2,0,1:T(8,128)(2,1)S(1)} all-to-all(bf16[72,32,128]{2,0,1:T(8,128)(2,1)S(1)} %bitcast.119), channel_id=1, replica_groups=mesh['section'=8,'expert'=8,'dp'=4] {'expert','dp'}, dimensions={1} | all-to-all | bytes 1179648 | tf_op jit(solution)/shard_map/while/body/eval_jaxpr/all_to_all | solution.py:47
  177.9 1.3 fusion.96
  179.2 1.7 collective-permute-start
  180.9 5.6 collective-permute-done
  188.4 63.6 %psum.50 = f32[256]{0:T(256)S(1)} all-reduce(f32[256]{0:T(256)S(1)} %fusion.92), channel_id=1, replica_groups=mesh['section'=8,'expert'=8,'dp'=4] {'expert','dp'}, use_global_device_ids=true, to_apply=%region_5.5 | all-reduce | flops 256 | bytes 2048 | tf_op jit(solution)/shard_map/while/body/eval_jaxpr/psum | solution.py:65
  253.0 63.6 %psum.51 = f32[256,8]{0,1:T(8,128)S(1)} all-reduce(f32[256,8]{0,1:T(8,128)S(1)} %fusion.93), channel_id=1, replica_groups=mesh['section'=8,'expert'=8,'dp'=4] {'expert','dp'}, use_global_device_ids=true, to_apply=%region_6.6 | all-reduce | flops 2048 | bytes 16384 | tf_op jit(solution)/shard_map/while/body/eval_jaxpr/psum | solution.py:69
  316.7 1.1 reduce-window.26
  319.9 15.9 %all_to_all.58 = bf16[32,72,128]{2,1,0:T(8,128)(2,1)S(1)} all-to-all(bf16[32,72,128]{2,1,0:T(8,128)(2,1)S(1)} %bitcast.117), channel_id=1, replica_groups=mesh['section'=8,'expert'=8,'dp'=4] {'expert','dp'}, dimensions={0} | all-to-all | bytes 1179648 | tf_op jit(solution)/shard_map/while/body/eval_jaxpr/all_to_all | solution.py:92
  336.6 4.4 fusion.95
  341.2 16.2 %all_to_all.59 = bf16[72,32,128]{2,0,1:T(8,128)(2,1)S(1)} all-to-all(bf16[72,32,128]{2,0,1:T(8,128)(2,1)S(1)} %bitcast.119), channel_id=1, replica_groups=mesh['section'=8,'expert'=8,'dp'=4] {'expert','dp'}, dimensions={1} | all-to-all | bytes 1179648 | tf_op jit(solution)/shard_map/while/body/eval_jaxpr/all_to_all | solution.py:47
  357.5 1.3 fusion.96
  358.9 4.3 collective-permute-done
  365.1 63.9 %psum.50 = f32[256]{0:T(256)S(1)} all-reduce(f32[256]{0:T(256)S(1)} %fusion.92), channel_id=1, replica_groups=mesh['section'=8,'expert'=8,'dp'=4] {'expert','dp'}, use_global_device_ids=true, to_apply=%region_5.5 | all-reduce | flops 256 | bytes 2048 | tf_op jit(solution)/shard_map/while/body/eval_jaxpr/psum | solution.py:65
  430.0 63.6 %psum.51 = f32[256,8]{0,1:T(8,128)S(1)} all-reduce(f32[256,8]{0,1:T(8,128)S(1)} %fusion.93), channel_id=1, replica_groups=mesh['section'=8,'expert'=8,'dp'=4] {'expert','dp'}, use_global_device_ids=true, to_apply=%region_6.6 | all-reduce | flops 2048 | bytes 16384 | tf_op jit(solution)/shard_map/while/body/eval_jaxpr/psum | solution.py:69
  493.7 1.1 reduce-window.26
  496.9 15.9 %all_to_all.58 = bf16[32,72,128]{2,1,0:T(8,128)(2,1)S(1)} all-to-all(bf16[32,72,128]{2,1,0:T(8,128)(2,1)S(1)} %bitcast.117), channel_id=1, replica_groups=mesh['section'=8,'expert'=8,'dp'=4] {'expert','dp'}, dimensions={0} | all-to-all | bytes 1179648 | tf_op jit(solution)/shard_map/while/body/eval_jaxpr/all_to_all | solution.py:92
  513.6 4.4 fusion.95
  518.2 16.2 %all_to_all.59 = bf16[72,32,128]{2,0,1:T(8,128)(2,1)S(1)} all-to-all(bf16[72,32,128]{2,0,1:T(8,128)(2,1)S(1)} %bitcast.119), channel_id=1, replica_groups=mesh['section'=8,'expert'=8,'dp'=4] {'expert','dp'}, dimensions={1} | all-to-all | bytes 1179648 | tf_op jit(solution)/shard_map/while/body/eval_jaxpr/all_to_all | solution.py:47
  534.5 1.3 fusion.96
  535.9 4.3 collective-permute-done
  542.1 63.9 %psum.50 = f32[256]{0:T(256)S(1)} all-reduce(f32[256]{0:T(256)S(1)} %fusion.92), channel_id=1, replica_groups=mesh['section'=8,'expert'=8,'dp'=4] {'expert','dp'}, use_global_device_ids=true, to_apply=%region_5.5 | all-reduce | flops 256 | bytes 2048 | tf_op jit(solution)/shard_map/while/body/eval_jaxpr/psum | solution.py:65
  607.0 63.6 %psum.51 = f32[256,8]{0,1:T(8,128)S(1)} all-reduce(f32[256,8]{0,1:T(8,128)S(1)} %fusion.93), channel_id=1, replica_groups=mesh['section'=8,'expert'=8,'dp'=4] {'expert','dp'}, use_global_device_ids=true, to_apply=%region_6.6 | all-reduce | flops 2048 | bytes 16384 | tf_op jit(solution)/shard_map/while/body/eval_jaxpr/psum | solution.py:69
  670.7 1.1 reduce-window.26
  673.9 15.9 %all_to_all.58 = bf16[32,72,128]{2,1,0:T(8,128)(2,1)S(1)} all-to-all(bf16[32,72,128]{2,1,0:T(8,128)(2,1)S(1)} %bitcast.117), channel_id=1, replica_groups=mesh['section'=8,'expert'=8,'dp'=4] {'expert','dp'}, dimensions={0} | all-to-all | bytes 1179648 | tf_op jit(solution)/shard_map/while/body/eval_jaxpr/all_to_all | solution.py:92
  690.6 4.4 fusion.95
  695.2 16.2 %all_to_all.59 = bf16[72,32,128]{2,0,1:T(8,128)(2,1)S(1)} all-to-all(bf16[72,32,128]{2,0,1:T(8,128)(2,1)S(1)} %bitcast.119), channel_id=1, replica_groups=mesh['section'=8,'expert'=8,'dp'=4] {'expert','dp'}, dimensions={1} | all-to-all | bytes 1179648 | tf_op jit(solution)/shard_map/while/body/eval_jaxpr/all_to_all | solution.py:47
  711.5 1.3 fusion.96
  712.9 4.3 collective-permute-done
  719.1 63.9 %psum.50 = f32[256]{0:T(256)S(1)} all-reduce(f32[256]{0:T(256)S(1)} %fusion.92), channel_id=1, replica_groups=mesh['section'=8,'expert'=8,'dp'=4] {'expert','dp'}, use_global_device_ids=true, to_apply=%region_5.5 | all-reduce | flops 256 | bytes 2048 | tf_op jit(solution)/shard_map/while/body/eval_jaxpr/psum | solution.py:65
  784.0 63.6 %psum.51 = f32[256,8]{0,1:T(8,128)S(1)} all-reduce(f32[256,8]{0,1:T(8,128)S(1)} %fusion.93), channel_id=1, replica_groups=mesh['section'=8,'expert'=8,'dp'=4] {'expert','dp'}, use_global_device_ids=true, to_apply=%region_6.6 | all-reduce | flops 2048 | bytes 16384 | tf_op jit(solution)/shard_map/while/body/eval_jaxpr/psum | solution.py:69
  847.7 1.1 reduce-window.26
  850.9 15.9 %all_to_all.58 = bf16[32,72,128]{2,1,0:T(8,128)(2,1)S(1)} all-to-all(bf16[32,72,128]{2,1,0:T(8,128)(2,1)S(1)} %bitcast.117), channel_id=1, replica_groups=mesh['section'=8,'expert'=8,'dp'=4] {'expert','dp'}, dimensions={0} | all-to-all | bytes 1179648 | tf_op jit(solution)/shard_map/while/body/eval_jaxpr/all_to_all | solution.py:92
  867.6 4.4 fusion.95
  872.2 16.2 %all_to_all.59 = bf16[72,32,128]{2,0,1:T(8,128)(2,1)S(1)} all-to-all(bf16[72,32,128]{2,0,1:T(8,128)(2,1)S(1)} %bitcast.119), channel_id=1, replica_groups=mesh['section'=8,'expert'=8,'dp'=4] {'expert','dp'}, dimensions={1} | all-to-all | bytes 1179648 | tf_op jit(solution)/shard_map/while/body/eval_jaxpr/all_to_all | solution.py:47
  888.5 1.3 fusion.96
  889.9 4.3 collective-permute-done
  896.1 63.9 %psum.50 = f32[256]{0:T(256)S(1)} all-reduce(f32[256]{0:T(256)S(1)} %fusion.92), channel_id=1, replica_groups=mesh['section'=8,'expert'=8,'dp'=4] {'expert','dp'}, use_global_device_ids=true, to_apply=%region_5.5 | all-reduce | flops 256 | bytes 2048 | tf_op jit(solution)/shard_map/while/body/eval_jaxpr/psum | solution.py:65
  960.9 63.6 %psum.51 = f32[256,8]{0,1:T(8,128)S(1)} all-reduce(f32[256,8]{0,1:T(8,128)S(1)} %fusion.93), channel_id=1, replica_groups=mesh['section'=8,'expert'=8,'dp'=4] {'expert','dp'}, use_global_device_ids=true, to_apply=%region_6.6 | all-reduce | flops 2048 | bytes 16384 | tf_op jit(solution)/shard_map/while/body/eval_jaxpr/psum | solution.py:69
  1027.9 15.9 %all_to_all.58 = bf16[32,72,128]{2,1,0:T(8,128)(2,1)S(1)} all-to-all(bf16[32,72,128]{2,1,0:T(8,128)(2,1)S(1)} %bitcast.117), channel_id=1, replica_groups=mesh['section'=8,'expert'=8,'dp'=4] {'expert','dp'}, dimensions={0} | all-to-all | bytes 1179648 | tf_op jit(solution)/shard_map/while/body/eval_jaxpr/all_to_all | solution.py:92
  1044.6 4.4 fusion.95
  1049.2 16.2 %all_to_all.59 = bf16[72,32,128]{2,0,1:T(8,128)(2,1)S(1)} all-to-all(bf16[72,32,128]{2,0,1:T(8,128)(2,1)S(1)} %bitcast.119), channel_id=1, replica_groups=mesh['section'=8,'expert'=8,'dp'=4] {'expert','dp'}, dimensions={1} | all-to-all | bytes 1179648 | tf_op jit(solution)/shard_map/while/body/eval_jaxpr/all_to_all | solution.py:47
  1065.5 1.3 fusion.96
  1066.9 4.3 collective-permute-done
  1073.1 63.9 %psum.50 = f32[256]{0:T(256)S(1)} all-reduce(f32[256]{0:T(256)S(1)} %fusion.92), channel_id=1, replica_groups=mesh['section'=8,'expert'=8,'dp'=4] {'expert','dp'}, use_global_device_ids=true, to_apply=%region_5.5 | all-reduce | flops 256 | bytes 2048 | tf_op jit(solution)/shard_map/while/body/eval_jaxpr/psum | solution.py:65
  1137.9 63.6 %psum.51 = f32[256,8]{0,1:T(8,128)S(1)} all-reduce(f32[256,8]{0,1:T(8,128)S(1)} %fusion.93), channel_id=1, replica_groups=mesh['section'=8,'expert'=8,'dp'=4] {'expert','dp'}, use_global_device_ids=true, to_apply=%region_6.6 | all-reduce | flops 2048 | bytes 16384 | tf_op jit(solution)/shard_map/while/body/eval_jaxpr/psum | solution.py:69
  1204.9 15.9 %all_to_all.58 = bf16[32,72,128]{2,1,0:T(8,128)(2,1)S(1)} all-to-all(bf16[32,72,128]{2,1,0:T(8,128)(2,1)S(1)} %bitcast.117), channel_id=1, replica_groups=mesh['section'=8,'expert'=8,'dp'=4] {'expert','dp'}, dimensions={0} | all-to-all | bytes 1179648 | tf_op jit(solution)/shard_map/while/body/eval_jaxpr/all_to_all | solution.py:92
  1221.6 4.4 fusion.95
  1226.2 16.2 %all_to_all.59 = bf16[72,32,128]{2,0,1:T(8,128)(2,1)S(1)} all-to-all(bf16[72,32,128]{2,0,1:T(8,128)(2,1)S(1)} %bitcast.119), channel_id=1, replica_groups=mesh['section'=8,'expert'=8,'dp'=4] {'expert','dp'}, dimensions={1} | all-to-all | bytes 1179648 | tf_op jit(solution)/shard_map/while/body/eval_jaxpr/all_to_all | solution.py:47
  1242.5 1.3 fusion.96
  1243.9 4.3 collective-permute-done
  1250.1 63.9 %psum.50 = f32[256]{0:T(256)S(1)} all-reduce(f32[256]{0:T(256)S(1)} %fusion.92), channel_id=1, replica_groups=mesh['section'=8,'expert'=8,'dp'=4] {'expert','dp'}, use_global_device_ids=true, to_apply=%region_5.5 | all-reduce | flops 256 | bytes 2048 | tf_op jit(solution)/shard_map/while/body/eval_jaxpr/psum | solution.py:65
  1314.9 63.6 %psum.51 = f32[256,8]{0,1:T(8,128)S(1)} all-reduce(f32[256,8]{0,1:T(8,128)S(1)} %fusion.93), channel_id=1, replica_groups=mesh['section'=8,'expert'=8,'dp'=4] {'expert','dp'}, use_global_device_ids=true, to_apply=%region_6.6 | all-reduce | flops 2048 | bytes 16384 | tf_op jit(solution)/shard_map/while/body/eval_jaxpr/psum | solution.py:69
  1381.8 15.9 %all_to_all.58 = bf16[32,72,128]{2,1,0:T(8,128)(2,1)S(1)} all-to-all(bf16[32,72,128]{2,1,0:T(8,128)(2,1)S(1)} %bitcast.117), channel_id=1, replica_groups=mesh['section'=8,'expert'=8,'dp'=4] {'expert','dp'}, dimensions={0} | all-to-all | bytes 1179648 | tf_op jit(solution)/shard_map/while/body/eval_jaxpr/all_to_all | solution.py:92
  1398.6 4.4 fusion.95
  1403.2 16.2 %all_to_all.59 = bf16[72,32,128]{2,0,1:T(8,128)(2,1)S(1)} all-to-all(bf16[72,32,128]{2,0,1:T(8,128)(2,1)S(1)} %bitcast.119), channel_id=1, replica_groups=mesh['section'=8,'expert'=8,'dp'=4] {'expert','dp'}, dimensions={1} | all-to-all | bytes 1179648 | tf_op jit(solution)/shard_map/while/body/eval_jaxpr/all_to_all | solution.py:47
  1419.5 1.3 fusion.96
  1420.9 4.3 collective-permute-done
  1425.4 72.8 %all-reduce = (f32[8]{0:T(128)S(1)}, f32[8]{0:T(128)S(1)}) all-reduce(f32[8]{0:T(128)S(1)} %broadcast_multiply_fusion.1, f32[8]{0:T(128)S(1)} %convolution_bitcast_fusion.1), channel_id=1, replica_groups=mesh['section'=8,'expert'=8,'dp'=4] {'section','expert','dp'}, use_global_device_ids=true, to_apply=%region_16.17 | all-reduce | flops 16 | bytes 128 | tf_op jit(solution)/shard_map/psum | solution.py:116
  (257 shorter events, 55.3 us)
Async XLA Ops:
  2.3 1422.9 %copy-start.1 = (bf16[1,256,128]{2,1,0:T(8,128)(2,1)S(1)}, bf16[1,256,128]{2,1,0:T(8,128)(2,1)}, u32[]{:S(2)}) copy-start(bf16[1,256,128]{2,1,0:T(8,128)(2,1)} %param.12) | copy-start | bytes 196612
  2.3 1423.0 %copy-start.3 = (s32[1,256]{1,0:T(1,128)S(1)}, s32[1,256]{1,0:T(1,128)}, u32[]{:S(2)}) copy-start(s32[1,256]{1,0:T(1,128)} %param.13) | copy-start | bytes 3076
  138.8 17.4 %copy-start = (bf16[4096,384]{1,0:T(8,128)(2,1)S(1)}, bf16[4096,384]{1,0:T(8,128)(2,1)}, u32[]{:S(2)}) copy-start(bf16[4096,384]{1,0:T(8,128)(2,1)} %get-tuple-element.482) | copy-start | bytes 9437188 | tf_op jit(solution)/shard_map/while
  179.2 7.3 collective-permute-start
  318.4 17.4 %copy-start = (bf16[4096,384]{1,0:T(8,128)(2,1)S(1)}, bf16[4096,384]{1,0:T(8,128)(2,1)}, u32[]{:S(2)}) copy-start(bf16[4096,384]{1,0:T(8,128)(2,1)} %get-tuple-element.482) | copy-start | bytes 9437188 | tf_op jit(solution)/shard_map/while
  358.8 4.4 collective-permute-start
  495.4 17.4 %copy-start = (bf16[4096,384]{1,0:T(8,128)(2,1)S(1)}, bf16[4096,384]{1,0:T(8,128)(2,1)}, u32[]{:S(2)}) copy-start(bf16[4096,384]{1,0:T(8,128)(2,1)} %get-tuple-element.482) | copy-start | bytes 9437188 | tf_op jit(solution)/shard_map/while
  535.8 4.4 collective-permute-start
  672.4 17.4 %copy-start = (bf16[4096,384]{1,0:T(8,128)(2,1)S(1)}, bf16[4096,384]{1,0:T(8,128)(2,1)}, u32[]{:S(2)}) copy-start(bf16[4096,384]{1,0:T(8,128)(2,1)} %get-tuple-element.482) | copy-start | bytes 9437188 | tf_op jit(solution)/shard_map/while
  712.8 4.4 collective-permute-start
  849.4 17.4 %copy-start = (bf16[4096,384]{1,0:T(8,128)(2,1)S(1)}, bf16[4096,384]{1,0:T(8,128)(2,1)}, u32[]{:S(2)}) copy-start(bf16[4096,384]{1,0:T(8,128)(2,1)} %get-tuple-element.482) | copy-start | bytes 9437188 | tf_op jit(solution)/shard_map/while
  889.8 4.4 collective-permute-start
  1026.4 17.4 %copy-start = (bf16[4096,384]{1,0:T(8,128)(2,1)S(1)}, bf16[4096,384]{1,0:T(8,128)(2,1)}, u32[]{:S(2)}) copy-start(bf16[4096,384]{1,0:T(8,128)(2,1)} %get-tuple-element.482) | copy-start | bytes 9437188 | tf_op jit(solution)/shard_map/while
  1066.8 4.4 collective-permute-start
  1203.4 17.4 %copy-start = (bf16[4096,384]{1,0:T(8,128)(2,1)S(1)}, bf16[4096,384]{1,0:T(8,128)(2,1)}, u32[]{:S(2)}) copy-start(bf16[4096,384]{1,0:T(8,128)(2,1)} %get-tuple-element.482) | copy-start | bytes 9437188 | tf_op jit(solution)/shard_map/while
  1243.8 4.4 collective-permute-start
  1380.4 17.4 %copy-start = (bf16[4096,384]{1,0:T(8,128)(2,1)S(1)}, bf16[4096,384]{1,0:T(8,128)(2,1)}, u32[]{:S(2)}) copy-start(bf16[4096,384]{1,0:T(8,128)(2,1)} %get-tuple-element.482) | copy-start | bytes 9437188 | tf_op jit(solution)/shard_map/while
  1420.8 4.4 collective-permute-start
  1498.9 1.5 copy-start.2
where the time goes:
time: 1500 us
  blocking collectives  1350 us (90%)
  matrix products  68.6 us (5%)
  waiting for transfers between devices  35.8 us (2%)
  local copies, waits for them, and re-layouts  20.9 us (1%)
  other arithmetic  16.5 us (1%)
    psum x8, blocking collectives, one_tick(): total_squares = lax.psum(local_squares, ('expert', 'dp'))  512 us
    psum x8, blocking collectives, one_tick(): logits = lax.psum(partial_logits, ('expert', 'dp'))  512 us
    all_to_all x8, blocking collectives, joined_work(): lax.all_to_all(expert_part.reshape(item_count, experts * lane_count, piec...  130 us
    all_to_all x8, blocking collectives, one_tick(): lax.all_to_all(spread.reshape(experts * lane_count, capacity, piece_width...  127 us
    psum x1, blocking collectives, per_device(): lax.psum((local_totals, local_counts), ('section', 'expert', 'dp'))  72.8 us
    ppermute x8, waiting for transfers between devices, from_behind(): return lax.ppermute(value, axis, pairs)  35.8 us
    dot_general x8, matrix products, expert_rows(): jnp.dot(activated, down_matrix, preferred_element_type=jnp.float32)  35.4 us
  transfers between devices with their start and end apart: 8, of which 8 were waited for; matrix products, arithmetic and copies ran while one was open for 0% of the time, Pallas kernels for 0%

commit v1 on v0

--- a/solution.py
+++ b/solution.py
@@ -66,7 +66,7 @@
         row_scale = lax.rsqrt(total_squares / full_width + 1e-06)[:, None]
         normed = (wide_state * row_scale * gain_row[None, :]).astype(jnp.bfloat16)
         partial_logits = jnp.dot(normed, router_block, preferred_element_type=jnp.float32)
-        logits = lax.psum(partial_logits, ("expert", "dp"))
+        logits = jnp.sum(lax.all_gather(partial_logits, ("expert", "dp")), axis=0)
         member = (choices[:, :, None] == expert_range[None, None, :]).astype(jnp.int32)
         flat_member = member.reshape(-1, experts)
         rank_before = jnp.cumsum(flat_member, axis=0) - flat_member

time: 1500 us -> 1300 us (0.87)
  blocking collectives: 1350 us -> 1140 us
    psum x8 -> x0, blocking collectives: 512 us -> none  [one_tick(): logits = lax.psum(partial_logits, ('expert', 'dp'))]
    all_gather x0 -> x8, blocking collectives: none -> 294 us  [one_tick(): logits = jnp.sum(lax.all_gather(partial_logits, ('expert', 'dp')), axis=0)]
where the time goes in v1:
time: 1300 us; the launch traced here: 1290 us
  blocking collectives  1140 us (88%)
  matrix products  81.5 us (6%)
  waiting for transfers between devices  35.8 us (3%)
  local copies, waits for them, and re-layouts  20.8 us (2%)
  other arithmetic  16.8 us (1%)
    psum x8, blocking collectives, one_tick(): total_squares = lax.psum(local_squares, ('expert', 'dp'))  512 us
    all_gather x8, blocking collectives, one_tick(): logits = jnp.sum(lax.all_gather(partial_logits, ('expert', 'dp')), axis=0)  294 us
    all_to_all x8, blocking collectives, joined_work(): lax.all_to_all(expert_part.reshape(item_count, experts * lane_count, piec...  130 us
    all_to_all x8, blocking collectives, one_tick(): lax.all_to_all(spread.reshape(experts * lane_count, capacity, piece_width...  127 us
    psum x1, blocking collectives, per_device(): lax.psum((local_totals, local_counts), ('section', 'expert', 'dp'))  72.8 us
    ppermute x8, waiting for transfers between devices, from_behind(): return lax.ppermute(value, axis, pairs)  35.8 us
    dot_general x8, matrix products, expert_rows(): jnp.dot(activated, down_matrix, preferred_element_type=jnp.float32)  34.9 us
  transfers between devices with their start and end apart: 8, of which 8 were waited for; matrix products, arithmetic and copies ran while one was open for 0% of the time, Pallas kernels for 0%

profile of v1, /device:TPU:1, one launch (start us, length us, event | category | flops | bytes accessed | tf_op | source)
XLA Modules:
  0.0 1294.9 jit_solution(5269389449176925619)
XLA Ops:
  2.3 1217.3 %while.17 = (s32[]{:T(128)}, bf16[256,128]{1,0:T(8,128)(2,1)S(1)}, s32[]{:T(128)}, s32[1,1,8,256,2]{3,4,2,1,0:T(2,128)}, f32[1,128]{1,0:T(1,128)}, /*index=5*/bf...) while((s32[]{:T(128)}, bf16[256,128]{1,0:T(8,128)(2,1)S(1)}, ...), condition=%wide.region_12.13_spmd.clone.clone, body=%wide.region_0.12_spmd.clone.clone.sunk | while | flops 947360128 | bytes 21585148 | solution.py:107
  4.3 65.3 %psum.33 = f32[256]{0:T(256)S(1)} all-reduce(f32[256]{0:T(256)S(1)} %fusion.92), channel_id=1, replica_groups=mesh['section'=8,'expert'=8,'dp'=4] {'expert','dp'}, use_global_device_ids=true, to_apply=%region_5.5 | all-reduce | flops 256 | bytes 2048 | tf_op jit(solution)/shard_map/while/body/eval_jaxpr/psum | solution.py:65
  72.2 39.3 %all-gather.3 = f32[8192,8]{0,1:T(8,128)S(1)} all-gather(f32[256,8]{0,1:T(8,128)S(1)} %fusion.93), channel_id=2, replica_groups=mesh['section'=8,'expert'=8,'dp'=4] {'expert','dp'}, dimensions={0}, use_global_device_ids=true | all-gather | bytes 270336 | tf_op jit(solution)/shard_map/while/body/eval_jaxpr/all_gather | solution.py:69
  112.9 15.8 %all_to_all.58 = bf16[32,72,128]{2,1,0:T(8,128)(2,1)S(1)} all-to-all(bf16[32,72,128]{2,1,0:T(8,128)(2,1)S(1)} %bitcast.120), channel_id=1, replica_groups=mesh['section'=8,'expert'=8,'dp'=4] {'expert','dp'}, dimensions={0} | all-to-all | bytes 1179648 | tf_op jit(solution)/shard_map/while/body/eval_jaxpr/all_to_all | solution.py:92
  128.8 2.5 fusion.94
  131.4 4.4 fusion.95
  135.9 16.2 %all_to_all.59 = bf16[72,32,128]{2,0,1:T(8,128)(2,1)S(1)} all-to-all(bf16[72,32,128]{2,0,1:T(8,128)(2,1)S(1)} %bitcast.122), channel_id=1, replica_groups=mesh['section'=8,'expert'=8,'dp'=4] {'expert','dp'}, dimensions={1} | all-to-all | bytes 1179648 | tf_op jit(solution)/shard_map/while/body/eval_jaxpr/all_to_all | solution.py:47
  152.2 1.3 fusion.96
  153.5 1.7 collective-permute-start
  155.2 5.6 collective-permute-done
  162.7 63.6 %psum.33 = f32[256]{0:T(256)S(1)} all-reduce(f32[256]{0:T(256)S(1)} %fusion.92), channel_id=1, replica_groups=mesh['section'=8,'expert'=8,'dp'=4] {'expert','dp'}, use_global_device_ids=true, to_apply=%region_5.5 | all-reduce | flops 256 | bytes 2048 | tf_op jit(solution)/shard_map/while/body/eval_jaxpr/psum | solution.py:65
  229.1 36.4 %all-gather.3 = f32[8192,8]{0,1:T(8,128)S(1)} all-gather(f32[256,8]{0,1:T(8,128)S(1)} %fusion.93), channel_id=2, replica_groups=mesh['section'=8,'expert'=8,'dp'=4] {'expert','dp'}, dimensions={0}, use_global_device_ids=true | all-gather | bytes 270336 | tf_op jit(solution)/shard_map/while/body/eval_jaxpr/all_gather | solution.py:69
  266.8 15.8 %all_to_all.58 = bf16[32,72,128]{2,1,0:T(8,128)(2,1)S(1)} all-to-all(bf16[32,72,128]{2,1,0:T(8,128)(2,1)S(1)} %bitcast.120), channel_id=1, replica_groups=mesh['section'=8,'expert'=8,'dp'=4] {'expert','dp'}, dimensions={0} | all-to-all | bytes 1179648 | tf_op jit(solution)/shard_map/while/body/eval_jaxpr/all_to_all | solution.py:92
  282.8 2.6 fusion.94
  285.3 4.4 fusion.95
  289.8 16.2 %all_to_all.59 = bf16[72,32,128]{2,0,1:T(8,128)(2,1)S(1)} all-to-all(bf16[72,32,128]{2,0,1:T(8,128)(2,1)S(1)} %bitcast.122), channel_id=1, replica_groups=mesh['section'=8,'expert'=8,'dp'=4] {'expert','dp'}, dimensions={1} | all-to-all | bytes 1179648 | tf_op jit(solution)/shard_map/while/body/eval_jaxpr/all_to_all | solution.py:47
  306.1 1.3 fusion.96
  307.5 4.3 collective-permute-done
  313.7 63.9 %psum.33 = f32[256]{0:T(256)S(1)} all-reduce(f32[256]{0:T(256)S(1)} %fusion.92), channel_id=1, replica_groups=mesh['section'=8,'expert'=8,'dp'=4] {'expert','dp'}, use_global_device_ids=true, to_apply=%region_5.5 | all-reduce | flops 256 | bytes 2048 | tf_op jit(solution)/shard_map/while/body/eval_jaxpr/psum | solution.py:65
  380.4 36.4 %all-gather.3 = f32[8192,8]{0,1:T(8,128)S(1)} all-gather(f32[256,8]{0,1:T(8,128)S(1)} %fusion.93), channel_id=2, replica_groups=mesh['section'=8,'expert'=8,'dp'=4] {'expert','dp'}, dimensions={0}, use_global_device_ids=true | all-gather | bytes 270336 | tf_op jit(solution)/shard_map/while/body/eval_jaxpr/all_gather | solution.py:69
  418.1 15.8 %all_to_all.58 = bf16[32,72,128]{2,1,0:T(8,128)(2,1)S(1)} all-to-all(bf16[32,72,128]{2,1,0:T(8,128)(2,1)S(1)} %bitcast.120), channel_id=1, replica_groups=mesh['section'=8,'expert'=8,'dp'=4] {'expert','dp'}, dimensions={0} | all-to-all | bytes 1179648 | tf_op jit(solution)/shard_map/while/body/eval_jaxpr/all_to_all | solution.py:92
  434.1 2.5 fusion.94
  436.6 4.4 fusion.95
  441.1 16.2 %all_to_all.59 = bf16[72,32,128]{2,0,1:T(8,128)(2,1)S(1)} all-to-all(bf16[72,32,128]{2,0,1:T(8,128)(2,1)S(1)} %bitcast.122), channel_id=1, replica_groups=mesh['section'=8,'expert'=8,'dp'=4] {'expert','dp'}, dimensions={1} | all-to-all | bytes 1179648 | tf_op jit(solution)/shard_map/while/body/eval_jaxpr/all_to_all | solution.py:47
  457.4 1.3 fusion.96
  458.8 4.3 collective-permute-done
  465.1 63.9 %psum.33 = f32[256]{0:T(256)S(1)} all-reduce(f32[256]{0:T(256)S(1)} %fusion.92), channel_id=1, replica_groups=mesh['section'=8,'expert'=8,'dp'=4] {'expert','dp'}, use_global_device_ids=true, to_apply=%region_5.5 | all-reduce | flops 256 | bytes 2048 | tf_op jit(solution)/shard_map/while/body/eval_jaxpr/psum | solution.py:65
  531.7 36.4 %all-gather.3 = f32[8192,8]{0,1:T(8,128)S(1)} all-gather(f32[256,8]{0,1:T(8,128)S(1)} %fusion.93), channel_id=2, replica_groups=mesh['section'=8,'expert'=8,'dp'=4] {'expert','dp'}, dimensions={0}, use_global_device_ids=true | all-gather | bytes 270336 | tf_op jit(solution)/shard_map/while/body/eval_jaxpr/all_gather | solution.py:69
  569.4 15.8 %all_to_all.58 = bf16[32,72,128]{2,1,0:T(8,128)(2,1)S(1)} all-to-all(bf16[32,72,128]{2,1,0:T(8,128)(2,1)S(1)} %bitcast.120), channel_id=1, replica_groups=mesh['section'=8,'expert'=8,'dp'=4] {'expert','dp'}, dimensions={0} | all-to-all | bytes 1179648 | tf_op jit(solution)/shard_map/while/body/eval_jaxpr/all_to_all | solution.py:92
  585.4 2.5 fusion.94
  587.9 4.4 fusion.95
  592.4 16.2 %all_to_all.59 = bf16[72,32,128]{2,0,1:T(8,128)(2,1)S(1)} all-to-all(bf16[72,32,128]{2,0,1:T(8,128)(2,1)S(1)} %bitcast.122), channel_id=1, replica_groups=mesh['section'=8,'expert'=8,'dp'=4] {'expert','dp'}, dimensions={1} | all-to-all | bytes 1179648 | tf_op jit(solution)/shard_map/while/body/eval_jaxpr/all_to_all | solution.py:47
  608.7 1.3 fusion.96
  610.1 4.3 collective-permute-done
  616.4 63.9 %psum.33 = f32[256]{0:T(256)S(1)} all-reduce(f32[256]{0:T(256)S(1)} %fusion.92), channel_id=1, replica_groups=mesh['section'=8,'expert'=8,'dp'=4] {'expert','dp'}, use_global_device_ids=true, to_apply=%region_5.5 | all-reduce | flops 256 | bytes 2048 | tf_op jit(solution)/shard_map/while/body/eval_jaxpr/psum | solution.py:65
  683.0 36.4 %all-gather.3 = f32[8192,8]{0,1:T(8,128)S(1)} all-gather(f32[256,8]{0,1:T(8,128)S(1)} %fusion.93), channel_id=2, replica_groups=mesh['section'=8,'expert'=8,'dp'=4] {'expert','dp'}, dimensions={0}, use_global_device_ids=true | all-gather | bytes 270336 | tf_op jit(solution)/shard_map/while/body/eval_jaxpr/all_gather | solution.py:69
  720.7 15.8 %all_to_all.58 = bf16[32,72,128]{2,1,0:T(8,128)(2,1)S(1)} all-to-all(bf16[32,72,128]{2,1,0:T(8,128)(2,1)S(1)} %bitcast.120), channel_id=1, replica_groups=mesh['section'=8,'expert'=8,'dp'=4] {'expert','dp'}, dimensions={0} | all-to-all | bytes 1179648 | tf_op jit(solution)/shard_map/while/body/eval_jaxpr/all_to_all | solution.py:92
  736.7 2.5 fusion.94
  739.2 4.4 fusion.95
  743.7 16.2 %all_to_all.59 = bf16[72,32,128]{2,0,1:T(8,128)(2,1)S(1)} all-to-all(bf16[72,32,128]{2,0,1:T(8,128)(2,1)S(1)} %bitcast.122), channel_id=1, replica_groups=mesh['section'=8,'expert'=8,'dp'=4] {'expert','dp'}, dimensions={1} | all-to-all | bytes 1179648 | tf_op jit(solution)/shard_map/while/body/eval_jaxpr/all_to_all | solution.py:47
  760.0 1.3 fusion.96
  761.4 4.3 collective-permute-done
  767.7 63.9 %psum.33 = f32[256]{0:T(256)S(1)} all-reduce(f32[256]{0:T(256)S(1)} %fusion.92), channel_id=1, replica_groups=mesh['section'=8,'expert'=8,'dp'=4] {'expert','dp'}, use_global_device_ids=true, to_apply=%region_5.5 | all-reduce | flops 256 | bytes 2048 | tf_op jit(solution)/shard_map/while/body/eval_jaxpr/psum | solution.py:65
  834.3 36.4 %all-gather.3 = f32[8192,8]{0,1:T(8,128)S(1)} all-gather(f32[256,8]{0,1:T(8,128)S(1)} %fusion.93), channel_id=2, replica_groups=mesh['section'=8,'expert'=8,'dp'=4] {'expert','dp'}, dimensions={0}, use_global_device_ids=true | all-gather | bytes 270336 | tf_op jit(solution)/shard_map/while/body/eval_jaxpr/all_gather | solution.py:69
  872.0 15.8 %all_to_all.58 = bf16[32,72,128]{2,1,0:T(8,128)(2,1)S(1)} all-to-all(bf16[32,72,128]{2,1,0:T(8,128)(2,1)S(1)} %bitcast.120), channel_id=1, replica_groups=mesh['section'=8,'expert'=8,'dp'=4] {'expert','dp'}, dimensions={0} | all-to-all | bytes 1179648 | tf_op jit(solution)/shard_map/while/body/eval_jaxpr/all_to_all | solution.py:92
  888.0 2.5 fusion.94
  890.5 4.4 fusion.95
  895.0 16.2 %all_to_all.59 = bf16[72,32,128]{2,0,1:T(8,128)(2,1)S(1)} all-to-all(bf16[72,32,128]{2,0,1:T(8,128)(2,1)S(1)} %bitcast.122), channel_id=1, replica_groups=mesh['section'=8,'expert'=8,'dp'=4] {'expert','dp'}, dimensions={1} | all-to-all | bytes 1179648 | tf_op jit(solution)/shard_map/while/body/eval_jaxpr/all_to_all | solution.py:47
  912.7 4.3 collective-permute-done
  919.0 63.9 %psum.33 = f32[256]{0:T(256)S(1)} all-reduce(f32[256]{0:T(256)S(1)} %fusion.92), channel_id=1, replica_groups=mesh['section'=8,'expert'=8,'dp'=4] {'expert','dp'}, use_global_device_ids=true, to_apply=%region_5.5 | all-reduce | flops 256 | bytes 2048 | tf_op jit(solution)/shard_map/while/body/eval_jaxpr/psum | solution.py:65
  985.6 36.4 %all-gather.3 = f32[8192,8]{0,1:T(8,128)S(1)} all-gather(f32[256,8]{0,1:T(8,128)S(1)} %fusion.93), channel_id=2, replica_groups=mesh['section'=8,'expert'=8,'dp'=4] {'expert','dp'}, dimensions={0}, use_global_device_ids=true | all-gather | bytes 270336 | tf_op jit(solution)/shard_map/while/body/eval_jaxpr/all_gather | solution.py:69
  1023.3 15.8 %all_to_all.58 = bf16[32,72,128]{2,1,0:T(8,128)(2,1)S(1)} all-to-all(bf16[32,72,128]{2,1,0:T(8,128)(2,1)S(1)} %bitcast.120), channel_id=1, replica_groups=mesh['section'=8,'expert'=8,'dp'=4] {'expert','dp'}, dimensions={0} | all-to-all | bytes 1179648 | tf_op jit(solution)/shard_map/while/body/eval_jaxpr/all_to_all | solution.py:92
  1039.3 2.5 fusion.94
  1041.8 4.4 fusion.95
  1046.3 16.2 %all_to_all.59 = bf16[72,32,128]{2,0,1:T(8,128)(2,1)S(1)} all-to-all(bf16[72,32,128]{2,0,1:T(8,128)(2,1)S(1)} %bitcast.122), channel_id=1, replica_groups=mesh['section'=8,'expert'=8,'dp'=4] {'expert','dp'}, dimensions={1} | all-to-all | bytes 1179648 | tf_op jit(solution)/shard_map/while/body/eval_jaxpr/all_to_all | solution.py:47
  1064.0 4.3 collective-permute-done
  1070.3 63.9 %psum.33 = f32[256]{0:T(256)S(1)} all-reduce(f32[256]{0:T(256)S(1)} %fusion.92), channel_id=1, replica_groups=mesh['section'=8,'expert'=8,'dp'=4] {'expert','dp'}, use_global_device_ids=true, to_apply=%region_5.5 | all-reduce | flops 256 | bytes 2048 | tf_op jit(solution)/shard_map/while/body/eval_jaxpr/psum | solution.py:65
  1136.9 36.4 %all-gather.3 = f32[8192,8]{0,1:T(8,128)S(1)} all-gather(f32[256,8]{0,1:T(8,128)S(1)} %fusion.93), channel_id=2, replica_groups=mesh['section'=8,'expert'=8,'dp'=4] {'expert','dp'}, dimensions={0}, use_global_device_ids=true | all-gather | bytes 270336 | tf_op jit(solution)/shard_map/while/body/eval_jaxpr/all_gather | solution.py:69
  1174.6 15.8 %all_to_all.58 = bf16[32,72,128]{2,1,0:T(8,128)(2,1)S(1)} all-to-all(bf16[32,72,128]{2,1,0:T(8,128)(2,1)S(1)} %bitcast.120), channel_id=1, replica_groups=mesh['section'=8,'expert'=8,'dp'=4] {'expert','dp'}, dimensions={0} | all-to-all | bytes 1179648 | tf_op jit(solution)/shard_map/while/body/eval_jaxpr/all_to_all | solution.py:92
  1190.6 2.5 fusion.94
  1193.1 4.4 fusion.95
  1197.6 16.2 %all_to_all.59 = bf16[72,32,128]{2,0,1:T(8,128)(2,1)S(1)} all-to-all(bf16[72,32,128]{2,0,1:T(8,128)(2,1)S(1)} %bitcast.122), channel_id=1, replica_groups=mesh['section'=8,'expert'=8,'dp'=4] {'expert','dp'}, dimensions={1} | all-to-all | bytes 1179648 | tf_op jit(solution)/shard_map/while/body/eval_jaxpr/all_to_all | solution.py:47
  1215.3 4.3 collective-permute-done
  1219.9 72.8 %all-reduce = (f32[8]{0:T(128)S(1)}, f32[8]{0:T(128)S(1)}) all-reduce(f32[8]{0:T(128)S(1)} %broadcast_multiply_fusion.1, f32[8]{0:T(128)S(1)} %convolution_bitcast_fusion.1), channel_id=1, replica_groups=mesh['section'=8,'expert'=8,'dp'=4] {'section','expert','dp'}, use_global_device_ids=true, to_apply=%region_16.17 | all-reduce | flops 16 | bytes 128 | tf_op jit(solution)/shard_map/psum | solution.py:116
  (249 shorter events, 58.0 us)
Async XLA Ops:
  2.3 1217.4 %copy-start = (bf16[1,256,128]{2,1,0:T(8,128)(2,1)S(1)}, bf16[1,256,128]{2,1,0:T(8,128)(2,1)}, u32[]{:S(2)}) copy-start(bf16[1,256,128]{2,1,0:T(8,128)(2,1)} %param.12) | copy-start | bytes 196612
  2.3 1217.5 %copy-start.2 = (s32[1,256]{1,0:T(1,128)S(1)}, s32[1,256]{1,0:T(1,128)}, u32[]{:S(2)}) copy-start(s32[1,256]{1,0:T(1,128)} %param.13) | copy-start | bytes 3076
  153.5 7.3 collective-permute-start
  307.4 4.4 collective-permute-start
  458.7 4.4 collective-permute-start
  610.0 4.4 collective-permute-start
  761.3 4.4 collective-permute-start
  912.6 4.4 collective-permute-start
  1063.9 4.4 collective-permute-start
  1215.2 4.4 collective-permute-start
  1293.3 1.5 copy-start.1
